TPU v7x, 32 devices: a whole 2x2x4 slice. The times are simulated.
32 devices in a mesh: groups: 2 (over x), long: 16 (over z, y, core).
Axes of the slice: x: 2, y: 2, z: 4, core: 2. Of those that a mesh axis runs over, the one named last changes fastest.
Arguments:
- displacement: float32 [4, 2, 128, 16, 256], P('groups', None, 'long'), parts along dimension 0, may hold values from -6 to 6
- velocity: float32 [4, 2, 128, 16, 256], P('groups', None, 'long'), parts along dimension 0, may hold values from -4 to 4
- damage: float32 [4, 128, 16, 256], P('groups', 'long'), parts along dimension 0, may hold values from 0 to 0.6
- material: int32 [4, 128, 16, 256], P('groups', 'long'), parts along dimension 0, may hold values from 0 to 3
- damage_table: float32 [2, 4], replicated, may hold values from 0.1 to 2
- fault_rows: int32 [4, 128, 16], P('groups', 'long'), parts along dimension 0, may hold values from 0 to 3
- kernel: float32 [16, 64, 2, 2], P(None, 'long'), may hold values from -1.5 to 1.5
- history: float32 [30, 64, 2, 2, 16], P('groups', 'long'), parts along dimension 0, may hold values from -6 to 6
Outputs:
- displacement_out: float32 [4, 2, 128, 16, 256], P('groups', None, 'long'), parts along dimension 0
- velocity_out: float32 [4, 2, 128, 16, 256], P('groups', None, 'long'), parts along dimension 0
- damage_out: float32 [4, 128, 16, 256], P('groups', 'long'), parts along dimension 0
- history_out: float32 [30, 64, 2, 2, 16], P('groups', 'long'), parts along dimension 0
There are 2 independent parts, one for each index of `groups`. A program takes and returns all parts, laid end to end along the dimension named above; an argument that names none is the same for every part. Nothing has to cross between parts.
Inputs may be any that keep to these rules, and one draw needn't show every extreme that they name: `fault_rows`: row of the fault face, counted from the fault.
All inputs are finite; a program needn't handle non-finite values.
Results may differ from a plain program's by a relative error of at most 0.00011.
Values sent between devices are 32-bit elements; how exact they have to be, the bound alone decides.
A program may use at most 64 MiB of HBM per device.

v0:
```python
import math
import jax
import jax.numpy as jnp
from jax import lax
from jax.sharding import PartitionSpec as P

STEPS = 2
time_step = 0.5


def padded_2(block, sides, width):
    for axis, dim in sides:
        count = lax.axis_size(axis)
        forward = [(i, i + 1) for i in range(count - 1)]
        forward.append((count - 1, 0))
        backward = [(target, source) for source, target in forward]
        low = lax.ppermute(
            lax.slice_in_dim(block, block.shape[dim] - width, None, axis=dim), axis, forward
        )
        high = lax.ppermute(lax.slice_in_dim(block, 0, width, axis=dim), axis, backward)
        block = jnp.concatenate([low, block, high], axis=dim)
    return block


def class_lookup(material, table_row):
    result = jnp.zeros(material.shape, table_row.dtype)
    for level in range(table_row.shape[0]):
        result = result + jnp.where(
            material == level, table_row[level], jnp.zeros((), table_row.dtype)
        )
    return result


def neighbour(values_in, axis, higher):
    selector = [slice(None)] * values_in.ndim
    for dimension in range(values_in.ndim - 3, values_in.ndim):
        selector[dimension] = slice(1, -1)
    selector[axis] = slice(2, None) if higher else slice(0, -2)
    return values_in[tuple(selector)]


def local_terms(padded_u, padded_c):
    outer_u = jnp.pad(padded_u, ((0, 0), (0, 0), (0, 0), (1, 1), (1, 1)))
    outer_c = jnp.pad(padded_c, ((0, 0), (0, 0), (1, 1), (1, 1)), mode="edge")
    centre_u = outer_u[:, :, 1:-1, 1:-1, 1:-1]
    centre_c = outer_c[:, 1:-1, 1:-1, 1:-1]
    forces = jnp.zeros_like(centre_u)
    energy = jnp.zeros_like(centre_c)
    for offset in range(3):
        above_u = neighbour(outer_u, 2 + offset, True)
        below_u = neighbour(outer_u, 2 + offset, False)
        above_c = neighbour(outer_c, 1 + offset, True)
        below_c = neighbour(outer_c, 1 + offset, False)
        forces = forces + (0.5 * (centre_c + above_c))[None] * (above_u - centre_u)
        forces = forces + (0.5 * (centre_c + below_c))[None] * (below_u - centre_u)
        gradient = 0.5 * (above_u - below_u)
        energy = energy + jnp.sum(gradient * gradient, axis=0)
    return (forces, energy)


def convolve(kernel, stacked):
    kernel_real = kernel[:, :, 0, :, None]
    kernel_imag = kernel[:, :, 1, :, None]
    spec_real = stacked[:, :, 0]
    spec_imag = stacked[:, :, 1]
    out_real = jnp.sum(kernel_real * spec_real - kernel_imag * spec_imag, axis=0)
    out_imag = jnp.sum(kernel_real * spec_imag + kernel_imag * spec_real, axis=0)
    return (out_real, out_imag)


def basis(waves, places, length):
    phase = (waves[:, None] * places[None, :] % length).astype(jnp.float32) * (
        2.0 * math.pi / length
    )
    return (jnp.cos(phase), jnp.sin(phase))


def spectral_terms(cosine, sine_table, slip_part, norming):
    part_real = (
        jnp.einsum("kx,cxz->kcz", cosine, slip_part, precision=lax.Precision.HIGHEST) * norming
    )
    part_imag = (
        -jnp.einsum("kx,cxz->kcz", sine_table, slip_part, precision=lax.Precision.HIGHEST) * norming
    )
    return jnp.stack([part_real, part_imag], 1)


def wave_sum(waves, places, spectrum, length, norming):
    cosine, sine_table = basis(waves, places, length)
    weights = jnp.where(waves == 0, 1.0, 2.0).astype(jnp.float32) * norming
    first_part = jnp.einsum(
        "kx,kcz->cxz", cosine * weights[:, None], spectrum[:, 0], precision=lax.Precision.HIGHEST
    )
    second_part = jnp.einsum(
        "kx,kcz->cxz",
        sine_table * weights[:, None],
        spectrum[:, 1],
        precision=lax.Precision.HIGHEST,
    )
    return first_part - second_part


def advance(
    disp_mid, vel_mid, dmg_mid, rate_mid, limit_mid, fault_mid, forces, energy, traction, signs
):
    pushes = traction[:, None, :, :, None] * signs[None] * fault_mid[None]
    vel_new = vel_mid + time_step * (forces + pushes)
    disp_new = disp_mid + time_step * vel_new
    dmg_new = 1.0 - (1.0 - dmg_mid) * jnp.exp(-rate_mid * jax.nn.softplus(energy - limit_mid))
    return (disp_new, vel_new, dmg_new)


def per_device(displacement, velocity, damage, material, damage_table, fault_rows, kernel, history):
    cells = displacement.shape[2]
    position = lax.axis_index("long")
    length = cells * lax.axis_size("long")
    owned = cells // 2
    norming = 1.0 / math.sqrt(length)
    rates = class_lookup(material, damage_table[0])
    limits = class_lookup(material, damage_table[1])
    heights = lax.broadcasted_iota(jnp.int32, damage.shape, 3)
    on_fault = (heights == fault_rows[..., None]).astype(displacement.dtype)
    signs = jnp.array([1.0, -1.0], displacement.dtype)[:, None, None, None]
    lagged = [history[level] for level in range(history.shape[0])]
    for number in range(STEPS):
        stiffness = 1.0 - damage
        stacked_fields = jnp.concatenate([displacement, stiffness[None]], 0)
        padded = padded_2(stacked_fields, (("long", 2),), 1)
        forces, energy = local_terms(padded[:-1], padded[-1])
        own_disp = displacement
        face = jnp.sum(own_disp * on_fault[None], axis=4)
        slip = face[:, 1] - face[:, 0]
        waves = jnp.arange(lax.axis_size("long") * owned, dtype=jnp.int32)
        places = position * cells + jnp.arange(cells, dtype=jnp.int32)
        cosine, sine_table = basis(waves, places, length)
        current = lax.psum_scatter(
            spectral_terms(cosine, sine_table, slip, norming),
            "long",
            scatter_dimension=0,
            tiled=True,
        )
        stacked_lags = jnp.stack([current] + lagged, 0)
        traction_real, traction_imag = convolve(kernel, stacked_lags)
        traction_spectrum = jnp.stack([traction_real, traction_imag], 1)

        def add_waves(piece):
            waves = jnp.arange(piece.shape[0], dtype=jnp.int32)
            places = position * cells + jnp.arange(cells, dtype=jnp.int32)
            return wave_sum(waves, places, piece, length, norming)

        traction = add_waves(lax.all_gather(traction_spectrum, "long", axis=0, tiled=True))
        displacement, velocity, damage = advance(
            displacement, velocity, damage, rates, limits, on_fault, forces, energy, traction, signs
        )
        lagged = [current] + lagged[:-1]
    return (displacement, velocity, damage, jnp.stack(lagged, 0))


def solution(mesh):
    placed = (
        P("groups", None, "long", None, None),
        P("groups", None, "long", None, None),
        P("groups", "long", None, None),
        P("groups", "long", None, None),
        P(),
        P("groups", "long", None),
        P(None, "long", None, None),
        P("groups", "long", None, None, None),
    )
    return jax.shard_map(
        per_device,
        mesh=mesh,
        in_specs=placed,
        out_specs=(
            P("groups", None, "long", None, None),
            P("groups", None, "long", None, None),
            P("groups", "long", None, None),
            P("groups", "long", None, None, None),
        ),
        check_vma=False,
    )
```

profile of v0, /device:TPU:0, one launch (start us, length us, event | category | flops | bytes accessed | tf_op | source)
XLA Modules:
  0.0 214.8 jit_solution(16481410820871778354)
XLA Ops:
  0.7 1.0 subtract_bitcast_fusion
  1.7 0.9 pad_maximum_fusion.31
  3.1 5.1 %collective-permute-start.1 = (f32[3,2,1,16,256]{4,3,2,1,0:T(8,128)S(1)}, f32[3,2,1,16,256]{4,3,2,1,0:T(8,128)S(1)}, u32[]{:S(2)}, u32[]{:S(2)}) collective-permute-start(f32[3,2,1,16,256]{4,3,2,1,0:T(8,128)S(1)} %get-tuple-element.28), channel_id=1, source_target_pairs={{1,0},{2,1},{3,2},{4,3},{5,4},{6,5},{7,6},{8,7},{9,8},{10,9},{11,1... | collective-permute-start | bytes 294920 | tf_op jit(solution)/shard_map/ppermute | solution.py:20
  8.8 0.7 fusion.127
  9.8 0.6 dynamic-slice
  11.5 1.4 multiply_reduce_fusion.5
  13.5 0.7 fusion.38
  14.3 0.9 fusion.122
  15.3 62.3 %all-reduce.2 = f32[64,2,2,16]{3,2,1,0:T(2,128)S(1)} all-reduce(f32[64,2,2,16]{3,2,1,0:T(2,128)S(1)} %copy.50), channel_id=2, replica_groups=mesh['groups'=2,'long'=16] {'long'}, use_global_device_ids=true, to_apply=%region_1.2.clone | all-reduce | flops 4096 | bytes 32768
  77.9 17.5 %all_gather.6 = f32[64,2,2,16]{3,2,1,0:T(2,128)S(1)} all-gather(f32[4,2,2,16]{3,2,1,0:T(2,128)S(1)} %copy.54), channel_id=1, replica_groups=mesh['groups'=2,'long'=16] {'long'}, dimensions={0}, use_global_device_ids=true | all-gather | bytes 17408 | tf_op jit(solution)/shard_map/all_gather | solution.py:151
  95.6 1.5 fusion.33
  97.8 6.1 %fusion.15 = (f32[2,8,16,256]{3,2,1,0:T(8,128)S(1)}, pred[2,8,16,256]{3,2,1,0:T(8,128)(4,1)}, pred[2,8,16,256]{3,2,1,0:T(8,128)(4,1)}, pred[2,8,16,256]{3,2,1,0:T(8,128)(4,1)}, pred[2,8,16,256]{3,2,1,0:T(8,128)(4,1)}) fusion(f32[2,8,16,256]{3,2,1,0:T(8,128)S(1)} %copy-done.5, f32[2,8,16,256]{3,2,1,0:T(8,128)S(1)} %copy-done.6, ...), kind=kLoop, calls=%fused_computation.57 | loop fusion | flops 2162688 | bytes 1835040 | tf_op jit(solution)/shard_map/sub | solution.py:126
  104.0 1.5 multiply_add_fusion.2
  105.9 4.1 %collective-permute-start.3 = (f32[3,2,1,16,256]{4,3,2,1,0:T(8,128)S(1)}, f32[3,2,1,16,256]{4,3,2,1,0:T(8,128)S(1)}, u32[]{:S(2)}, u32[]{:S(2)}) collective-permute-start(f32[3,2,1,16,256]{4,3,2,1,0:T(8,128)S(1)} %get-tuple-element.26), channel_id=1, source_target_pairs={{1,0},{2,1},{3,2},{4,3},{5,4},{6,5},{7,6},{8,7},{9,8},{10,9},{11,1... | collective-permute-start | bytes 294920 | tf_op jit(solution)/shard_map/ppermute | solution.py:20
  110.0 0.6 slice.347
  110.7 1.8 collective-permute-done.2
  112.5 0.7 fusion.28
  113.2 0.9 multiply_reduce_fusion.2
  115.1 1.3 multiply_reduce_fusion.1
  116.5 0.8 fusion.121
  117.2 0.8 copy.57
  118.0 63.8 %all-reduce.3 = f32[64,2,2,16]{3,2,1,0:T(2,128)} all-reduce(f32[64,2,2,16]{3,2,1,0:T(2,128)} %copy.57), channel_id=3, replica_groups=mesh['groups'=2,'long'=16] {'long'}, use_global_device_ids=true, to_apply=%region_8.9.clone | all-reduce | flops 4096 | bytes 32768
  181.8 0.7 dynamic-slice_bitcast_fusion
  182.8 17.5 %all_gather.7 = f32[64,2,2,16]{3,2,1,0:T(2,128)S(1)} all-gather(f32[4,2,2,16]{3,2,1,0:T(2,128)S(1)} %copy.61), channel_id=1, replica_groups=mesh['groups'=2,'long'=16] {'long'}, dimensions={0}, use_global_device_ids=true | all-gather | bytes 17408 | tf_op jit(solution)/shard_map/all_gather | solution.py:151
  200.3 0.7 fusion.125
  200.9 0.9 copy.72
  201.8 0.9 fusion.45
  202.9 0.9 fusion.9
  203.9 1.7 pad_maximum_fusion.27
  205.6 1.3 fusion.23
  207.0 6.2 %fusion.19 = f32[2,8,16,256]{3,2,1,0:T(8,128)} fusion(f32[2,8,16,256]{3,2,1,0:T(8,128)S(1)} %get-tuple-element.18, f32[2,8,16,256]{3,2,1,0:T(8,128)S(1)} %copy-done.9, f32[2,8,16,256]{3,2,1,0:T(8,128)S(1)} %copy-done.10, f32[2,8,16,256]{3,2,1,0:T(8,128)S(1)} %copy-done.8, pred[2,8,16,256]{3,2,1,0:T(8,128)(4,1)S(1)} %copy-done.20, ...), kind=kLoop, calls=%fused_computation.61 | loop fusion | flops 1769472 | bytes 1572896 | tf_op jit(solution)/shard_map/sub | solution.py:109
  213.2 1.6 multiply_add_fusion
  (103 shorter events, 6.0 us)
Async XLA Ops:
  0.6 9.1 %copy-start.27 = (u32[32]{0:T(128)S(1)}, u32[32]{0:T(128)}, u32[]{:S(2)}) copy-start(u32[32]{0:T(128)} %constant.74) | copy-start | bytes 388
  0.6 10.4 %copy-start = (f32[2,2,8,16,256]{4,3,2,1,0:T(8,128)S(1)}, f32[2,2,8,16,256]{4,3,2,1,0:T(8,128)}, u32[]{:S(2)}) copy-start(f32[2,2,8,16,256]{4,3,2,1,0:T(8,128)} %param.9) | copy-start | bytes 1572868
  0.7 8.1 %copy-start.24 = (s32[2,8,16]{2,1,0:T(8,128)S(1)}, s32[2,8,16]{2,1,0:T(8,128)}, u32[]{:S(2)}) copy-start(s32[2,8,16]{2,1,0:T(8,128)} %param.14) | copy-start | bytes 3076
  0.7 8.2 %copy-start.23 = (f32[2,4]{1,0:T(2,128)S(1)}, f32[2,4]{1,0:T(2,128)}, u32[]{:S(2)}) copy-start(f32[2,4]{1,0:T(2,128)} %param.13) | copy-start | bytes 100
  0.7 8.8 %copy-start.25 = (f32[16,4,2,2]{0,3,2,1:T(2,128)S(1)}, f32[16,4,2,2]{0,3,2,1:T(2,128)}, u32[]{:S(2)}) copy-start(f32[16,4,2,2]{0,3,2,1:T(2,128)} %param.15) | copy-start | bytes 3076
  2.6 8.4 %collective-permute-start = (f32[3,2,1,16,256]{4,3,2,1,0:T(8,128)S(1)}, f32[3,2,1,16,256]{4,3,2,1,0:T(8,128)S(1)}, u32[]{:S(2)}, u32[]{:S(2)}) collective-permute-start(f32[3,2,1,16,256]{4,3,2,1,0:T(8,128)S(1)} %get-tuple-element.27), channel_id=1, source_target_pairs={{0,1},{1,2},{2,3},{3,4},{4,5},{5,6},{6,7},{7,8},{8,9},{9,10},{10,1... | collective-permute-start | bytes 294920 | tf_op jit(solution)/shard_map/ppermute | solution.py:17
  3.1 7.9 %collective-permute-start.1 = (f32[3,2,1,16,256]{4,3,2,1,0:T(8,128)S(1)}, f32[3,2,1,16,256]{4,3,2,1,0:T(8,128)S(1)}, u32[]{:S(2)}, u32[]{:S(2)}) collective-permute-start(f32[3,2,1,16,256]{4,3,2,1,0:T(8,128)S(1)} %get-tuple-element.28), channel_id=1, source_target_pairs={{1,0},{2,1},{3,2},{4,3},{5,4},{6,5},{7,6},{8,7},{9,8},{10,9},{11,1... | collective-permute-start | bytes 294920 | tf_op jit(solution)/shard_map/ppermute | solution.py:20
  9.7 67.9 %copy-start.14 = (f32[16,4,2]{2,1,0:T(4,128)}, f32[16,4,2]{2,1,0:T(4,128)S(1)}, u32[]{:S(2)}) copy-start(f32[16,4,2]{2,1,0:T(4,128)S(1)} %copy.53) | copy-start | bytes 1540
  13.5 64.1 %copy-start.11 = (f32[15,4,2,2,16]{4,3,2,1,0:T(2,128)S(1)}, f32[15,4,2,2,16]{4,3,2,1,0:T(2,128)}, u32[]{:S(2)}) copy-start(f32[15,4,2,2,16]{4,3,2,1,0:T(2,128)} %param.16) | copy-start | bytes 46084
  95.4 2.3 %copy-start.26 = (f32[2]{0:T(128)S(1)}, f32[2]{0:T(128)}, u32[]{:S(2)}) copy-start(f32[2]{0:T(128)} %constant.60.clone) | copy-start | bytes 28
  95.6 2.2 %copy-start.4 = (f32[2,8,16,256]{3,2,1,0:T(8,128)S(1)}, f32[2,8,16,256]{3,2,1,0:T(8,128)}, u32[]{:S(2)}) copy-start(f32[2,8,16,256]{3,2,1,0:T(8,128)} %get-tuple-element.6) | copy-start | bytes 786436
  95.6 2.2 %copy-start.5 = (f32[2,8,16,256]{3,2,1,0:T(8,128)S(1)}, f32[2,8,16,256]{3,2,1,0:T(8,128)}, u32[]{:S(2)}) copy-start(f32[2,8,16,256]{3,2,1,0:T(8,128)} %get-tuple-element.7) | copy-start | bytes 786436
  95.6 2.2 %copy-start.6 = (f32[2,8,16,256]{3,2,1,0:T(8,128)S(1)}, f32[2,8,16,256]{3,2,1,0:T(8,128)}, u32[]{:S(2)}) copy-start(f32[2,8,16,256]{3,2,1,0:T(8,128)} %get-tuple-element.62) | copy-start | bytes 786436
  95.6 2.2 %copy-start.7 = (f32[2,8,16,256]{3,2,1,0:T(8,128)S(1)}, f32[2,8,16,256]{3,2,1,0:T(8,128)}, u32[]{:S(2)}) copy-start(f32[2,8,16,256]{3,2,1,0:T(8,128)} %param.11) | copy-start | bytes 786436
  97.1 6.9 %copy-start.3 = (f32[2,8,16,256]{3,2,1,0:T(8,128)S(1)}, f32[2,8,16,256]{3,2,1,0:T(8,128)}, u32[]{:S(2)}) copy-start(f32[2,8,16,256]{3,2,1,0:T(8,128)} %fusion.38) | copy-start | bytes 786436
  97.1 6.9 %copy-start.13 = (f32[2,2,8,16,256]{4,3,2,1,0:T(8,128)S(1)}, f32[2,2,8,16,256]{4,3,2,1,0:T(8,128)}, u32[]{:S(2)}) copy-start(f32[2,2,8,16,256]{4,3,2,1,0:T(8,128)} %param.10) | copy-start | bytes 1572868
  104.0 6.0 %copy-start.12 = (f32[15,4,2,2,16]{4,3,2,1,0:T(2,128)S(1)}, f32[15,4,2,2,16]{4,3,2,1,0:T(2,128)}, u32[]{:S(2)}) copy-start(f32[15,4,2,2,16]{4,3,2,1,0:T(2,128)} %param.16) | copy-start | bytes 46084
  105.5 6.9 %collective-permute-start.2 = (f32[3,2,1,16,256]{4,3,2,1,0:T(8,128)S(1)}, f32[3,2,1,16,256]{4,3,2,1,0:T(8,128)S(1)}, u32[]{:S(2)}, u32[]{:S(2)}) collective-permute-start(f32[3,2,1,16,256]{4,3,2,1,0:T(8,128)S(1)} %get-tuple-element.25), channel_id=1, source_target_pairs={{0,1},{1,2},{2,3},{3,4},{4,5},{5,6},{6,7},{7,8},{8,9},{9,10},{10,1... | collective-permute-start | bytes 294920 | tf_op jit(solution)/shard_map/ppermute | solution.py:17
  105.9 6.5 %collective-permute-start.3 = (f32[3,2,1,16,256]{4,3,2,1,0:T(8,128)S(1)}, f32[3,2,1,16,256]{4,3,2,1,0:T(8,128)S(1)}, u32[]{:S(2)}, u32[]{:S(2)}) collective-permute-start(f32[3,2,1,16,256]{4,3,2,1,0:T(8,128)S(1)} %get-tuple-element.26), channel_id=1, source_target_pairs={{1,0},{2,1},{3,2},{4,3},{5,4},{6,5},{7,6},{8,7},{9,8},{10,9},{11,1... | collective-permute-start | bytes 294920 | tf_op jit(solution)/shard_map/ppermute | solution.py:20
  112.5 3.9 %copy-start.21 = (f32[2,10,1,256]{3,2,1,0:T(1,128)}, f32[2,10,1,256]{3,2,1,0:T(1,128)S(1)}, u32[]{:S(2)}) copy-start(f32[2,10,1,256]{3,2,1,0:T(1,128)S(1)} %get-tuple-element.43) | copy-start | bytes 61444
  112.5 3.9 %copy-start.22 = (f32[2,10,1,256]{3,2,1,0:T(1,128)}, f32[2,10,1,256]{3,2,1,0:T(1,128)S(1)}, u32[]{:S(2)}) copy-start(f32[2,10,1,256]{3,2,1,0:T(1,128)S(1)} %get-tuple-element.44) | copy-start | bytes 61444
  116.4 66.1 %slice-start = ((f32[15,4,2,2,16]{4,3,2,1,0:T(2,128)}), f32[14,4,2,2,16]{4,3,2,1,0:T(2,128)S(1)}, s32[]{:S(2)}) async-start(f32[15,4,2,2,16]{4,3,2,1,0:T(2,128)} %param.16), calls=%async_computation | async-start | bytes 229376 | tf_op jit(solution)/shard_map/slice | solution.py:124
  116.4 66.2 %copy-start.15 = (f32[16,4,2]{2,1,0:T(4,128)S(1)}, f32[16,4,2]{2,1,0:T(4,128)}, u32[]{:S(2)}) copy-start(f32[16,4,2]{2,1,0:T(4,128)} %copy-done.14) | copy-start | bytes 1540
  203.9 3.1 %copy-start.8 = (f32[2,8,16,256]{3,2,1,0:T(8,128)S(1)}, f32[2,8,16,256]{3,2,1,0:T(8,128)}, u32[]{:S(2)}) copy-start(f32[2,8,16,256]{3,2,1,0:T(8,128)} %get-tuple-element.4) | copy-start | bytes 786436
  203.9 3.1 %copy-start.9 = (f32[2,8,16,256]{3,2,1,0:T(8,128)S(1)}, f32[2,8,16,256]{3,2,1,0:T(8,128)}, u32[]{:S(2)}) copy-start(f32[2,8,16,256]{3,2,1,0:T(8,128)} %get-tuple-element.5) | copy-start | bytes 786436
  203.9 3.1 %copy-start.10 = (f32[2,8,16,256]{3,2,1,0:T(8,128)S(1)}, f32[2,8,16,256]{3,2,1,0:T(8,128)}, u32[]{:S(2)}) copy-start(f32[2,8,16,256]{3,2,1,0:T(8,128)} %get-tuple-element.8) | copy-start | bytes 786436
  203.9 3.1 %copy-start.17 = (pred[2,8,16,256]{3,2,1,0:T(8,128)(4,1)S(1)}, pred[2,8,16,256]{3,2,1,0:T(8,128)(4,1)}, u32[]{:S(2)}) copy-start(pred[2,8,16,256]{3,2,1,0:T(8,128)(4,1)} %get-tuple-element.19) | copy-start | bytes 196612
  203.9 3.1 %copy-start.18 = (pred[2,8,16,256]{3,2,1,0:T(8,128)(4,1)S(1)}, pred[2,8,16,256]{3,2,1,0:T(8,128)(4,1)}, u32[]{:S(2)}) copy-start(pred[2,8,16,256]{3,2,1,0:T(8,128)(4,1)} %get-tuple-element.20) | copy-start | bytes 196612
  203.9 3.1 %copy-start.19 = (pred[2,8,16,256]{3,2,1,0:T(8,128)(4,1)S(1)}, pred[2,8,16,256]{3,2,1,0:T(8,128)(4,1)}, u32[]{:S(2)}) copy-start(pred[2,8,16,256]{3,2,1,0:T(8,128)(4,1)} %get-tuple-element.21) | copy-start | bytes 196612
  203.9 3.1 %copy-start.20 = (pred[2,8,16,256]{3,2,1,0:T(8,128)(4,1)S(1)}, pred[2,8,16,256]{3,2,1,0:T(8,128)(4,1)}, u32[]{:S(2)}) copy-start(pred[2,8,16,256]{3,2,1,0:T(8,128)(4,1)} %get-tuple-element.22) | copy-start | bytes 196612
  206.9 6.3 %copy-start.1 = (f32[2,2,8,16,256]{4,3,2,1,0:T(8,128)S(1)}, f32[2,2,8,16,256]{4,3,2,1,0:T(8,128)}, u32[]{:S(2)}) copy-start(f32[2,2,8,16,256]{4,3,2,1,0:T(8,128)} %get-tuple-element.24) | copy-start | bytes 1572868
  207.0 6.3 %copy-start.2 = (f32[2,8,16,256]{3,2,1,0:T(8,128)S(1)}, f32[2,8,16,256]{3,2,1,0:T(8,128)}, u32[]{:S(2)}) copy-start(f32[2,8,16,256]{3,2,1,0:T(8,128)} %fusion.28) | copy-start | bytes 786436
  (2 other events, 3.9 us)
where the time goes:
time: 215 us
  blocking collectives  161 us (75%)
  other arithmetic  29.3 us (14%)
  starting transfers between devices  10.1 us (5%)
  local copies, waits for them, and re-layouts  7.45 us (3%)
  matrix products  3.4 us (2%)
    unnamed x2, blocking collectives  126 us
    all_gather x2, blocking collectives, per_device(): lax.all_gather(traction_spectrum, 'long', axis=0, tiled=True)  35 us
    ppermute x2, starting transfers between devices, padded_2(): lax.ppermute(lax.slice_in_dim(block, 0, width, axis=dim), axis, backward)  9.16 us
    sub x1, other arithmetic, advance(): 1.0 - (1.0 - dmg_mid) * jnp.exp(-rate_mid * jax.nn.softplus(energy - limi...  6.16 us
    sub x1, other arithmetic, per_device(): stiffness = 1.0 - damage  6.15 us
  transfers between devices with their start and end apart: 4, of which 1 were waited for; matrix products, arithmetic and copies ran while one was open for 1% of the time, Pallas kernels for 0%

commit v1 on v0

--- a/solution.py
+++ b/solution.py
@@ -6,6 +6,28 @@
 
 STEPS = 2
 time_step = 0.5
+
+
+def in_order(blocks, dim):
+    blocks = jnp.moveaxis(blocks, 0, dim)
+    lengths = blocks.shape
+    return blocks.reshape(*lengths[:dim], lengths[dim] * lengths[dim + 1], *lengths[dim + 2 :])
+
+
+def collect(x, axis, dim):
+    size = lax.axis_size(axis)
+    pairs = [(i, (i + 1) % size) for i in range(size)]
+    back = [(b, a) for a, b in pairs]
+    lower, upper = ([], [])
+    for step in range(size - 1):
+        if step % 2 == 0:
+            lower.append(lax.ppermute(lower[-1] if lower else x, axis, pairs))
+        else:
+            upper.append(lax.ppermute(upper[-1] if upper else x, axis, back))
+    tiles = jnp.stack([*lower[::-1], x, *upper])
+    shift = lax.axis_index(axis) - len(lower)
+    tiles = tiles[(jnp.arange(size) - shift) % size]
+    return in_order(tiles, dim)
 
 
 def padded_2(block, sides, width):
@@ -148,7 +170,7 @@
             places = position * cells + jnp.arange(cells, dtype=jnp.int32)
             return wave_sum(waves, places, piece, length, norming)
 
-        traction = add_waves(lax.all_gather(traction_spectrum, "long", axis=0, tiled=True))
+        traction = add_waves(collect(traction_spectrum, "long", 0))
         displacement, velocity, damage = advance(
             displacement, velocity, damage, rates, limits, on_fault, forces, energy, traction, signs
         )

time: 215 us -> 273 us (1.27)
  starting transfers between devices: 10.1 us -> 72.4 us
  blocking collectives: 161 us -> 125 us
  waiting for transfers between devices: 1.76 us -> 20.9 us
  local copies, waits for them, and re-layouts: 7.45 us -> 17.4 us
  other arithmetic: 29.3 us -> 33.1 us
    ppermute x0 -> x30, starting transfers between devices: none -> 62.3 us  [the longest x14 62.1 us: collect(): upper.append(lax.ppermute(upper[-1] if upper else x, axis, back))]
    all_gather x2 -> x0, blocking collectives: 35 us -> none  [per_device(): lax.all_gather(traction_spectrum, 'long', axis=0, tiled=True)]
    ppermute x0 -> x30, waiting for transfers between devices: none -> 18.6 us  [the longest x16 13.8 us: collect(): lower.append(lax.ppermute(lower[-1] if lower else x, axis, pairs))]
    unnamed x63 -> x57, local copies, waits for them, and re-layouts: 1.91 us -> 9.15 us
    gather x0 -> x4, local copies, waits for them, and re-layouts: none -> 4.13 us  [collect(): tiles = tiles[(jnp.arange(size) - shift) % size]]
  transfers between devices with their start and end apart: 4 -> 34, of which waited for: 1 -> 16; matrix products, arithmetic and copies ran while one was open for 1% -> 11% of each run, Pallas kernels for 0% -> 0%
where the time goes in v1:
time: 273 us
  blocking collectives  125 us (46%)
  starting transfers between devices  72.4 us (27%)
  other arithmetic  33.1 us (12%)
  waiting for transfers between devices  20.9 us (8%)
  local copies, waits for them, and re-layouts  17.4 us (6%)
    unnamed x2, blocking collectives  125 us
    ppermute x14, starting transfers between devices, collect(): upper.append(lax.ppermute(upper[-1] if upper else x, axis, back))  62.1 us
    ppermute x16, waiting for transfers between devices, collect(): lower.append(lax.ppermute(lower[-1] if lower else x, axis, pairs))  13.8 us
    ppermute x2, starting transfers between devices, padded_2(): lax.ppermute(lax.slice_in_dim(block, 0, width, axis=dim), axis, backward)  9.52 us
    unnamed x57, local copies, waits for them, and re-layouts  9.15 us
    sub x1, other arithmetic, per_device(): stiffness = 1.0 - damage  7.19 us
    sub x1, other arithmetic, advance(): 1.0 - (1.0 - dmg_mid) * jnp.exp(-rate_mid * jax.nn.softplus(energy - limi...  6.1 us
    add x2, other arithmetic, advance(): disp_new = disp_mid + time_step * vel_new  5.86 us
  transfers between devices with their start and end apart: 34, of which 16 were waited for; matrix products, arithmetic and copies ran while one was open for 11% of the time, Pallas kernels for 0%

profile of v1, /device:TPU:0, one launch (start us, length us, event | category | flops | bytes accessed | tf_op | source)
XLA Modules:
  0.0 272.6 jit_solution(18168414912511501956)
XLA Ops:
  3.1 5.1 %collective-permute-start.1 = (f32[3,2,1,16,256]{4,3,2,1,0:T(8,128)S(1)}, f32[3,2,1,16,256]{4,3,2,1,0:T(8,128)S(1)}, u32[]{:S(2)}, u32[]{:S(2)}) collective-permute-start(f32[3,2,1,16,256]{4,3,2,1,0:T(8,128)S(1)} %get-tuple-element.28), channel_id=1, source_target_pairs={{1,0},{2,1},{3,2},{4,3},{5,4},{6,5},{7,6},{8,7},{9,8},{10,9},{11,1... | collective-permute-start | bytes 294920 | tf_op jit(solution)/shard_map/ppermute | solution.py:42
  12.2 1.3 multiply_reduce_fusion.5
  15.5 62.1 %all-reduce.2 = f32[64,2,2,16]{3,2,1,0:T(2,128)} all-reduce(f32[64,2,2,16]{3,2,1,0:T(2,128)S(1)} %copy.45), channel_id=2, replica_groups=mesh['groups'=2,'long'=16] {'long'}, use_global_device_ids=true, to_apply=%region_1.2.clone | all-reduce | flops 4096 | bytes 32768
  79.4 4.4 %collective-permute-start.10 = (f32[4,2,2,16]{3,2,0,1:T(2,128)S(1)}, f32[4,2,2,16]{3,2,0,1:T(2,128)S(1)}, u32[]{:S(2)}, u32[]{:S(2)}) collective-permute-start(f32[4,2,2,16]{3,2,0,1:T(2,128)S(1)} %pad_maximum_fusion.35), channel_id=1, source_target_pairs={{1,0},{2,1},{3,2},{4,3},{5,4},{6,5},{7,6},{8,7},{9,8},{10,9},{11,1... | collective-permute-start | bytes 3080 | tf_op jit(solution)/shard_map/ppermute | solution.py:26
  83.9 1.3 collective-permute-done.2
  85.2 7.2 %fusion.15 = (f32[2,8,16,256]{3,2,1,0:T(8,128)S(1)}, pred[2,8,16,256]{3,2,1,0:T(8,128)(4,1)}, pred[2,8,16,256]{3,2,1,0:T(8,128)(4,1)}, pred[2,8,16,256]{3,2,1,0:T(8,128)(4,1)}, pred[2,8,16,256]{3,2,1,0:T(8,128)(4,1)}) fusion(f32[2,8,16,256]{3,2,1,0:T(8,128)S(1)} %get-tuple-element.7, f32[2,8,16,256]{3,2,1,0:T(8,128)} %get-tuple-element.58, ...), kind=kLoop, calls=%fused_computation.59 | loop fusion | flops 2162688 | bytes 1835040 | tf_op jit(solution)/shard_map/sub | solution.py:148
  92.4 4.5 %collective-permute-start.11 = (f32[4,2,2,16]{3,2,0,1:T(2,128)S(1)}, f32[4,2,2,16]{3,2,0,1:T(2,128)S(1)}, u32[]{:S(2)}, u32[]{:S(2)}) collective-permute-start(f32[4,2,2,16]{3,2,0,1:T(2,128)S(1)} %collective-permute-done.10), channel_id=1, source_target_pairs={{1,0},{2,1},{3,2},{4,3},{5,4},{6,5},{7,6},{8,7},{9,8},{10,9},{11,1... | collective-permute-start | bytes 3080 | tf_op jit(solution)/shard_map/ppermute | solution.py:26
  96.9 1.2 collective-permute-done.4
  98.3 4.4 %collective-permute-start.12 = (f32[4,2,2,16]{3,2,0,1:T(2,128)S(1)}, f32[4,2,2,16]{3,2,0,1:T(2,128)S(1)}, u32[]{:S(2)}, u32[]{:S(2)}) collective-permute-start(f32[4,2,2,16]{3,2,0,1:T(2,128)S(1)} %collective-permute-done.11), channel_id=1, source_target_pairs={{1,0},{2,1},{3,2},{4,3},{5,4},{6,5},{7,6},{8,7},{9,8},{10,9},{11,1... | collective-permute-start | bytes 3080 | tf_op jit(solution)/shard_map/ppermute | solution.py:26
  102.7 1.2 collective-permute-done.5
  104.1 4.4 %collective-permute-start.13 = (f32[4,2,2,16]{3,2,0,1:T(2,128)S(1)}, f32[4,2,2,16]{3,2,0,1:T(2,128)S(1)}, u32[]{:S(2)}, u32[]{:S(2)}) collective-permute-start(f32[4,2,2,16]{3,2,0,1:T(2,128)S(1)} %collective-permute-done.12), channel_id=1, source_target_pairs={{1,0},{2,1},{3,2},{4,3},{5,4},{6,5},{7,6},{8,7},{9,8},{10,9},{11,1... | collective-permute-start | bytes 3080 | tf_op jit(solution)/shard_map/ppermute | solution.py:26
  109.9 4.5 %collective-permute-start.14 = (f32[4,2,2,16]{3,2,0,1:T(2,128)S(1)}, f32[4,2,2,16]{3,2,0,1:T(2,128)S(1)}, u32[]{:S(2)}, u32[]{:S(2)}) collective-permute-start(f32[4,2,2,16]{3,2,0,1:T(2,128)S(1)} %collective-permute-done.13), channel_id=1, source_target_pairs={{1,0},{2,1},{3,2},{4,3},{5,4},{6,5},{7,6},{8,7},{9,8},{10,9},{11,1... | collective-permute-start | bytes 3080 | tf_op jit(solution)/shard_map/ppermute | solution.py:26
  115.5 1.3 fusion.33
  116.8 4.4 %collective-permute-start.15 = (f32[4,2,2,16]{3,2,0,1:T(2,128)S(1)}, f32[4,2,2,16]{3,2,0,1:T(2,128)S(1)}, u32[]{:S(2)}, u32[]{:S(2)}) collective-permute-start(f32[4,2,2,16]{3,2,0,1:T(2,128)S(1)} %collective-permute-done.14), channel_id=1, source_target_pairs={{1,0},{2,1},{3,2},{4,3},{5,4},{6,5},{7,6},{8,7},{9,8},{10,9},{11,1... | collective-permute-start | bytes 3080 | tf_op jit(solution)/shard_map/ppermute | solution.py:26
  122.6 4.4 %collective-permute-start.16 = (f32[4,2,2,16]{3,2,0,1:T(2,128)S(1)}, f32[4,2,2,16]{3,2,0,1:T(2,128)S(1)}, u32[]{:S(2)}, u32[]{:S(2)}) collective-permute-start(f32[4,2,2,16]{3,2,0,1:T(2,128)S(1)} %collective-permute-done.15), channel_id=1, source_target_pairs={{1,0},{2,1},{3,2},{4,3},{5,4},{6,5},{7,6},{8,7},{9,8},{10,9},{11,1... | collective-permute-start | bytes 3080 | tf_op jit(solution)/shard_map/ppermute | solution.py:26
  129.9 3.0 %multiply_add_fusion.2 = (f32[2,2,8,16,256]{4,3,2,1,0:T(8,128)S(1)}, f32[2,2,8,16,256]{4,3,2,1,0:T(8,128)}) fusion(f32[2,2,8,16,256]{4,3,2,1,0:T(8,128)S(1)} %copy-done, f32[2,2,8,16,256]{4,3,2,1,0:T(8,128)} %param.10, f32[2,8,16,256]{3,2,1,0:T(8,128)S(1)} %fusion.40, f32[2,2,8,16]{3,2,1,0:T(8,128)S(1)} %broadcast_multiply_fusion.1, ...), kind=kLoop, calls=%fused_computation.48 | loop fusion | flops 3538944 | bytes 6490112 | tf_op jit(solution)/shard_map/add | solution.py:130
  132.9 4.5 %collective-permute-start.18 = (f32[3,2,1,16,256]{4,3,2,1,0:T(8,128)S(1)}, f32[3,2,1,16,256]{4,3,2,1,0:T(8,128)S(1)}, u32[]{:S(2)}, u32[]{:S(2)}) collective-permute-start(f32[3,2,1,16,256]{4,3,2,1,0:T(8,128)S(1)} %get-tuple-element.26), channel_id=1, source_target_pairs={{1,0},{2,1},{3,2},{4,3},{5,4},{6,5},{7,6},{8,7},{9,8},{10,9},{11,1... | collective-permute-start | bytes 294920 | tf_op jit(solution)/shard_map/ppermute | solution.py:42
  137.4 2.3 collective-permute-done.17
  141.2 62.8 %all-reduce.3 = f32[64,2,2,16]{3,2,1,0:T(2,128)S(1)} all-reduce(f32[64,2,2,16]{3,2,1,0:T(2,128)S(1)} %copy.52), channel_id=3, replica_groups=mesh['groups'=2,'long'=16] {'long'}, use_global_device_ids=true, to_apply=%region_8.9.clone | all-reduce | flops 4096 | bytes 32768
  204.4 4.4 %collective-permute-start.27 = (f32[4,2,2,16]{3,2,0,1:T(2,128)S(1)}, f32[4,2,2,16]{3,2,0,1:T(2,128)S(1)}, u32[]{:S(2)}, u32[]{:S(2)}) collective-permute-start(f32[4,2,2,16]{3,2,0,1:T(2,128)S(1)} %pad_maximum_fusion.36), channel_id=1, source_target_pairs={{1,0},{2,1},{3,2},{4,3},{5,4},{6,5},{7,6},{8,7},{9,8},{10,9},{11,1... | collective-permute-start | bytes 3080 | tf_op jit(solution)/shard_map/ppermute | solution.py:26
  210.2 5.7 %collective-permute-done.20 = f32[4,2,2,16]{3,2,0,1:T(2,128)S(1)} collective-permute-done((f32[4,2,2,16]{3,2,0,1:T(2,128)S(1)}, f32[4,2,2,16]{3,2,0,1:T(2,128)S(1)}, u32[]{:S(2)}, u32[]{:S(2)}) %collective-permute-start.20) | collective-permute-done | bytes 1056 | tf_op jit(solution)/shard_map/ppermute | solution.py:24
  216.1 4.5 %collective-permute-start.28 = (f32[4,2,2,16]{3,2,0,1:T(2,128)S(1)}, f32[4,2,2,16]{3,2,0,1:T(2,128)S(1)}, u32[]{:S(2)}, u32[]{:S(2)}) collective-permute-start(f32[4,2,2,16]{3,2,0,1:T(2,128)S(1)} %collective-permute-done.27), channel_id=1, source_target_pairs={{1,0},{2,1},{3,2},{4,3},{5,4},{6,5},{7,6},{8,7},{9,8},{10,9},{11,1... | collective-permute-start | bytes 3080 | tf_op jit(solution)/shard_map/ppermute | solution.py:26
  221.7 1.4 fusion.23
  223.1 4.5 %collective-permute-start.29 = (f32[4,2,2,16]{3,2,0,1:T(2,128)S(1)}, f32[4,2,2,16]{3,2,0,1:T(2,128)S(1)}, u32[]{:S(2)}, u32[]{:S(2)}) collective-permute-start(f32[4,2,2,16]{3,2,0,1:T(2,128)S(1)} %collective-permute-done.28), channel_id=1, source_target_pairs={{1,0},{2,1},{3,2},{4,3},{5,4},{6,5},{7,6},{8,7},{9,8},{10,9},{11,1... | collective-permute-start | bytes 3080 | tf_op jit(solution)/shard_map/ppermute | solution.py:26
  229.0 4.4 %collective-permute-start.30 = (f32[4,2,2,16]{3,2,0,1:T(2,128)S(1)}, f32[4,2,2,16]{3,2,0,1:T(2,128)S(1)}, u32[]{:S(2)}, u32[]{:S(2)}) collective-permute-start(f32[4,2,2,16]{3,2,0,1:T(2,128)S(1)} %collective-permute-done.29), channel_id=1, source_target_pairs={{1,0},{2,1},{3,2},{4,3},{5,4},{6,5},{7,6},{8,7},{9,8},{10,9},{11,1... | collective-permute-start | bytes 3080 | tf_op jit(solution)/shard_map/ppermute | solution.py:26
  233.4 6.1 %fusion.19 = f32[2,8,16,256]{3,2,1,0:T(8,128)} fusion(f32[2,8,16,256]{3,2,1,0:T(8,128)S(1)} %get-tuple-element.18, f32[2,8,16,256]{3,2,1,0:T(8,128)S(1)} %get-tuple-element.5, f32[2,8,16,256]{3,2,1,0:T(8,128)S(1)} %copy-done.2, f32[2,8,16,256]{3,2,1,0:T(8,128)S(1)} %get-tuple-element.4, pred[2,8,16,256]{3,2,1,0:T(8,128)(4,1)S(1)} %copy-done.8, ...), kind=kLoop, calls=%fused_computation.63 | loop fusion | flops 1769472 | bytes 1572896 | tf_op jit(solution)/shard_map/sub | solution.py:131
  239.6 4.4 %collective-permute-start.31 = (f32[4,2,2,16]{3,2,0,1:T(2,128)S(1)}, f32[4,2,2,16]{3,2,0,1:T(2,128)S(1)}, u32[]{:S(2)}, u32[]{:S(2)}) collective-permute-start(f32[4,2,2,16]{3,2,0,1:T(2,128)S(1)} %collective-permute-done.30), channel_id=1, source_target_pairs={{1,0},{2,1},{3,2},{4,3},{5,4},{6,5},{7,6},{8,7},{9,8},{10,9},{11,1... | collective-permute-start | bytes 3080 | tf_op jit(solution)/shard_map/ppermute | solution.py:26
  244.0 1.3 collective-permute-done.31
  245.3 4.4 %collective-permute-start.32 = (f32[4,2,2,16]{3,2,0,1:T(2,128)S(1)}, f32[4,2,2,16]{3,2,0,1:T(2,128)S(1)}, u32[]{:S(2)}, u32[]{:S(2)}) collective-permute-start(f32[4,2,2,16]{3,2,0,1:T(2,128)S(1)} %collective-permute-done.31), channel_id=1, source_target_pairs={{1,0},{2,1},{3,2},{4,3},{5,4},{6,5},{7,6},{8,7},{9,8},{10,9},{11,1... | collective-permute-start | bytes 3080 | tf_op jit(solution)/shard_map/ppermute | solution.py:26
  251.1 4.4 %collective-permute-start.33 = (f32[4,2,2,16]{3,2,0,1:T(2,128)S(1)}, f32[4,2,2,16]{3,2,0,1:T(2,128)S(1)}, u32[]{:S(2)}, u32[]{:S(2)}) collective-permute-start(f32[4,2,2,16]{3,2,0,1:T(2,128)S(1)} %collective-permute-done.32), channel_id=1, source_target_pairs={{1,0},{2,1},{3,2},{4,3},{5,4},{6,5},{7,6},{8,7},{9,8},{10,9},{11,1... | collective-permute-start | bytes 3080 | tf_op jit(solution)/shard_map/ppermute | solution.py:26
  265.1 2.3 gather_fusion.1
  269.7 2.9 %multiply_add_fusion = (f32[2,2,8,16,256]{4,3,2,1,0:T(8,128)}, f32[2,2,8,16,256]{4,3,2,1,0:T(8,128)}) fusion(f32[2,2,8,16,256]{4,3,2,1,0:T(8,128)S(1)} %get-tuple-element.23, f32[2,2,8,16,256]{4,3,2,1,0:T(8,128)S(1)} %copy-done.1, f32[2,8,16,256]{3,2,1,0:T(8,128)S(1)} %fusion.40, f32[2,2,8,16]{3,2,1,0:T(8,128)S(1)} %broadcast_multiply_fusion, ...), kind=kLoop, calls=%fused_computation.42 | loop fusion | flops 3538944 | bytes 6490112 | tf_op jit(solution)/shard_map/add | solution.py:130
  (162 shorter events, 35.6 us)
Async XLA Ops:
  2.6 9.1 %collective-permute-start = (f32[3,2,1,16,256]{4,3,2,1,0:T(8,128)S(1)}, f32[3,2,1,16,256]{4,3,2,1,0:T(8,128)S(1)}, u32[]{:S(2)}, u32[]{:S(2)}) collective-permute-start(f32[3,2,1,16,256]{4,3,2,1,0:T(8,128)S(1)} %get-tuple-element.27), channel_id=1, source_target_pairs={{0,1},{1,2},{2,3},{3,4},{4,5},{5,6},{6,7},{7,8},{8,9},{9,10},{10,1... | collective-permute-start | bytes 294920 | tf_op jit(solution)/shard_map/ppermute | solution.py:39
  3.1 8.6 %collective-permute-start.1 = (f32[3,2,1,16,256]{4,3,2,1,0:T(8,128)S(1)}, f32[3,2,1,16,256]{4,3,2,1,0:T(8,128)S(1)}, u32[]{:S(2)}, u32[]{:S(2)}) collective-permute-start(f32[3,2,1,16,256]{4,3,2,1,0:T(8,128)S(1)} %get-tuple-element.28), channel_id=1, source_target_pairs={{1,0},{2,1},{3,2},{4,3},{5,4},{6,5},{7,6},{8,7},{9,8},{10,9},{11,1... | collective-permute-start | bytes 294920 | tf_op jit(solution)/shard_map/ppermute | solution.py:42
  79.4 5.8 %collective-permute-start.2 = (f32[4,2,2,16]{3,2,0,1:T(2,128)S(1)}, f32[4,2,2,16]{3,2,0,1:T(2,128)S(1)}, u32[]{:S(2)}, u32[]{:S(2)}) collective-permute-start(f32[4,2,2,16]{3,2,0,1:T(2,128)S(1)} %pad_maximum_fusion.35), channel_id=1, source_target_pairs={{0,1},{1,2},{2,3},{3,4},{4,5},{5,6},{6,7},{7,8},{8,9},{9,10},{10,1... | collective-permute-start | bytes 3080 | tf_op jit(solution)/shard_map/ppermute | solution.py:24
  79.4 13.0 %collective-permute-start.10 = (f32[4,2,2,16]{3,2,0,1:T(2,128)S(1)}, f32[4,2,2,16]{3,2,0,1:T(2,128)S(1)}, u32[]{:S(2)}, u32[]{:S(2)}) collective-permute-start(f32[4,2,2,16]{3,2,0,1:T(2,128)S(1)} %pad_maximum_fusion.35), channel_id=1, source_target_pairs={{1,0},{2,1},{3,2},{4,3},{5,4},{6,5},{7,6},{8,7},{9,8},{10,9},{11,1... | collective-permute-start | bytes 3080 | tf_op jit(solution)/shard_map/ppermute | solution.py:26
  85.2 7.2 %collective-permute-start.3 = (f32[4,2,2,16]{3,2,0,1:T(2,128)S(1)}, f32[4,2,2,16]{3,2,0,1:T(2,128)S(1)}, u32[]{:S(2)}, u32[]{:S(2)}) collective-permute-start(f32[4,2,2,16]{3,2,0,1:T(2,128)S(1)} %collective-permute-done.2), channel_id=1, source_target_pairs={{0,1},{1,2},{2,3},{3,4},{4,5},{5,6},{6,7},{7,8},{8,9},{9,10},{10,1... | collective-permute-start | bytes 3080 | tf_op jit(solution)/shard_map/ppermute | solution.py:24
  92.4 5.8 %collective-permute-start.4 = (f32[4,2,2,16]{3,2,0,1:T(2,128)S(1)}, f32[4,2,2,16]{3,2,0,1:T(2,128)S(1)}, u32[]{:S(2)}, u32[]{:S(2)}) collective-permute-start(f32[4,2,2,16]{3,2,0,1:T(2,128)S(1)} %collective-permute-done.3), channel_id=1, source_target_pairs={{0,1},{1,2},{2,3},{3,4},{4,5},{5,6},{6,7},{7,8},{8,9},{9,10},{10,1... | collective-permute-start | bytes 3080 | tf_op jit(solution)/shard_map/ppermute | solution.py:24
  92.4 5.9 %collective-permute-start.11 = (f32[4,2,2,16]{3,2,0,1:T(2,128)S(1)}, f32[4,2,2,16]{3,2,0,1:T(2,128)S(1)}, u32[]{:S(2)}, u32[]{:S(2)}) collective-permute-start(f32[4,2,2,16]{3,2,0,1:T(2,128)S(1)} %collective-permute-done.10), channel_id=1, source_target_pairs={{1,0},{2,1},{3,2},{4,3},{5,4},{6,5},{7,6},{8,7},{9,8},{10,9},{11,1... | collective-permute-start | bytes 3080 | tf_op jit(solution)/shard_map/ppermute | solution.py:26
  98.3 5.8 %collective-permute-start.12 = (f32[4,2,2,16]{3,2,0,1:T(2,128)S(1)}, f32[4,2,2,16]{3,2,0,1:T(2,128)S(1)}, u32[]{:S(2)}, u32[]{:S(2)}) collective-permute-start(f32[4,2,2,16]{3,2,0,1:T(2,128)S(1)} %collective-permute-done.11), channel_id=1, source_target_pairs={{1,0},{2,1},{3,2},{4,3},{5,4},{6,5},{7,6},{8,7},{9,8},{10,9},{11,1... | collective-permute-start | bytes 3080 | tf_op jit(solution)/shard_map/ppermute | solution.py:26
  103.9 5.8 %collective-permute-start.6 = (f32[4,2,2,16]{3,2,0,1:T(2,128)S(1)}, f32[4,2,2,16]{3,2,0,1:T(2,128)S(1)}, u32[]{:S(2)}, u32[]{:S(2)}) collective-permute-start(f32[4,2,2,16]{3,2,0,1:T(2,128)S(1)} %collective-permute-done.5), channel_id=1, source_target_pairs={{0,1},{1,2},{2,3},{3,4},{4,5},{5,6},{6,7},{7,8},{8,9},{9,10},{10,1... | collective-permute-start | bytes 3080 | tf_op jit(solution)/shard_map/ppermute | solution.py:24
  104.1 5.8 %collective-permute-start.13 = (f32[4,2,2,16]{3,2,0,1:T(2,128)S(1)}, f32[4,2,2,16]{3,2,0,1:T(2,128)S(1)}, u32[]{:S(2)}, u32[]{:S(2)}) collective-permute-start(f32[4,2,2,16]{3,2,0,1:T(2,128)S(1)} %collective-permute-done.12), channel_id=1, source_target_pairs={{1,0},{2,1},{3,2},{4,3},{5,4},{6,5},{7,6},{8,7},{9,8},{10,9},{11,1... | collective-permute-start | bytes 3080 | tf_op jit(solution)/shard_map/ppermute | solution.py:26
  109.7 5.8 %collective-permute-start.7 = (f32[4,2,2,16]{3,2,0,1:T(2,128)S(1)}, f32[4,2,2,16]{3,2,0,1:T(2,128)S(1)}, u32[]{:S(2)}, u32[]{:S(2)}) collective-permute-start(f32[4,2,2,16]{3,2,0,1:T(2,128)S(1)} %collective-permute-done.6), channel_id=1, source_target_pairs={{0,1},{1,2},{2,3},{3,4},{4,5},{5,6},{6,7},{7,8},{8,9},{9,10},{10,1... | collective-permute-start | bytes 3080 | tf_op jit(solution)/shard_map/ppermute | solution.py:24
  109.9 6.9 %collective-permute-start.14 = (f32[4,2,2,16]{3,2,0,1:T(2,128)S(1)}, f32[4,2,2,16]{3,2,0,1:T(2,128)S(1)}, u32[]{:S(2)}, u32[]{:S(2)}) collective-permute-start(f32[4,2,2,16]{3,2,0,1:T(2,128)S(1)} %collective-permute-done.13), channel_id=1, source_target_pairs={{1,0},{2,1},{3,2},{4,3},{5,4},{6,5},{7,6},{8,7},{9,8},{10,9},{11,1... | collective-permute-start | bytes 3080 | tf_op jit(solution)/shard_map/ppermute | solution.py:26
  115.5 5.8 %collective-permute-start.8 = (f32[4,2,2,16]{3,2,0,1:T(2,128)S(1)}, f32[4,2,2,16]{3,2,0,1:T(2,128)S(1)}, u32[]{:S(2)}, u32[]{:S(2)}) collective-permute-start(f32[4,2,2,16]{3,2,0,1:T(2,128)S(1)} %collective-permute-done.7), channel_id=1, source_target_pairs={{0,1},{1,2},{2,3},{3,4},{4,5},{5,6},{6,7},{7,8},{8,9},{9,10},{10,1... | collective-permute-start | bytes 3080 | tf_op jit(solution)/shard_map/ppermute | solution.py:24
  116.8 5.8 %collective-permute-start.15 = (f32[4,2,2,16]{3,2,0,1:T(2,128)S(1)}, f32[4,2,2,16]{3,2,0,1:T(2,128)S(1)}, u32[]{:S(2)}, u32[]{:S(2)}) collective-permute-start(f32[4,2,2,16]{3,2,0,1:T(2,128)S(1)} %collective-permute-done.14), channel_id=1, source_target_pairs={{1,0},{2,1},{3,2},{4,3},{5,4},{6,5},{7,6},{8,7},{9,8},{10,9},{11,1... | collective-permute-start | bytes 3080 | tf_op jit(solution)/shard_map/ppermute | solution.py:26
  121.3 5.8 %collective-permute-start.9 = (f32[4,2,2,16]{3,2,0,1:T(2,128)S(1)}, f32[4,2,2,16]{3,2,0,1:T(2,128)S(1)}, u32[]{:S(2)}, u32[]{:S(2)}) collective-permute-start(f32[4,2,2,16]{3,2,0,1:T(2,128)S(1)} %collective-permute-done.8), channel_id=1, source_target_pairs={{0,1},{1,2},{2,3},{3,4},{4,5},{5,6},{6,7},{7,8},{8,9},{9,10},{10,1... | collective-permute-start | bytes 3080 | tf_op jit(solution)/shard_map/ppermute | solution.py:24
  122.6 5.8 %collective-permute-start.16 = (f32[4,2,2,16]{3,2,0,1:T(2,128)S(1)}, f32[4,2,2,16]{3,2,0,1:T(2,128)S(1)}, u32[]{:S(2)}, u32[]{:S(2)}) collective-permute-start(f32[4,2,2,16]{3,2,0,1:T(2,128)S(1)} %collective-permute-done.15), channel_id=1, source_target_pairs={{1,0},{2,1},{3,2},{4,3},{5,4},{6,5},{7,6},{8,7},{9,8},{10,9},{11,1... | collective-permute-start | bytes 3080 | tf_op jit(solution)/shard_map/ppermute | solution.py:26
  132.8 6.8 %collective-permute-start.17 = (f32[3,2,1,16,256]{4,3,2,1,0:T(8,128)S(1)}, f32[3,2,1,16,256]{4,3,2,1,0:T(8,128)S(1)}, u32[]{:S(2)}, u32[]{:S(2)}) collective-permute-start(f32[3,2,1,16,256]{4,3,2,1,0:T(8,128)S(1)} %get-tuple-element.25), channel_id=1, source_target_pairs={{0,1},{1,2},{2,3},{3,4},{4,5},{5,6},{6,7},{7,8},{8,9},{9,10},{10,1... | collective-permute-start | bytes 294920 | tf_op jit(solution)/shard_map/ppermute | solution.py:39
  132.9 6.7 %collective-permute-start.18 = (f32[3,2,1,16,256]{4,3,2,1,0:T(8,128)S(1)}, f32[3,2,1,16,256]{4,3,2,1,0:T(8,128)S(1)}, u32[]{:S(2)}, u32[]{:S(2)}) collective-permute-start(f32[3,2,1,16,256]{4,3,2,1,0:T(8,128)S(1)} %get-tuple-element.26), channel_id=1, source_target_pairs={{1,0},{2,1},{3,2},{4,3},{5,4},{6,5},{7,6},{8,7},{9,8},{10,9},{11,1... | collective-permute-start | bytes 294920 | tf_op jit(solution)/shard_map/ppermute | solution.py:42
  204.3 5.8 %collective-permute-start.19 = (f32[4,2,2,16]{3,2,0,1:T(2,128)S(1)}, f32[4,2,2,16]{3,2,0,1:T(2,128)S(1)}, u32[]{:S(2)}, u32[]{:S(2)}) collective-permute-start(f32[4,2,2,16]{3,2,0,1:T(2,128)S(1)} %pad_maximum_fusion.36), channel_id=1, source_target_pairs={{0,1},{1,2},{2,3},{3,4},{4,5},{5,6},{6,7},{7,8},{8,9},{9,10},{10,1... | collective-permute-start | bytes 3080 | tf_op jit(solution)/shard_map/ppermute | solution.py:24
  204.4 11.7 %collective-permute-start.27 = (f32[4,2,2,16]{3,2,0,1:T(2,128)S(1)}, f32[4,2,2,16]{3,2,0,1:T(2,128)S(1)}, u32[]{:S(2)}, u32[]{:S(2)}) collective-permute-start(f32[4,2,2,16]{3,2,0,1:T(2,128)S(1)} %pad_maximum_fusion.36), channel_id=1, source_target_pairs={{1,0},{2,1},{3,2},{4,3},{5,4},{6,5},{7,6},{8,7},{9,8},{10,9},{11,1... | collective-permute-start | bytes 3080 | tf_op jit(solution)/shard_map/ppermute | solution.py:26
  210.2 5.8 %collective-permute-start.20 = (f32[4,2,2,16]{3,2,0,1:T(2,128)S(1)}, f32[4,2,2,16]{3,2,0,1:T(2,128)S(1)}, u32[]{:S(2)}, u32[]{:S(2)}) collective-permute-start(f32[4,2,2,16]{3,2,0,1:T(2,128)S(1)} %collective-permute-done.19), channel_id=1, source_target_pairs={{0,1},{1,2},{2,3},{3,4},{4,5},{5,6},{6,7},{7,8},{8,9},{9,10},{10,1... | collective-permute-start | bytes 3080 | tf_op jit(solution)/shard_map/ppermute | solution.py:24
  215.9 5.8 %collective-permute-start.21 = (f32[4,2,2,16]{3,2,0,1:T(2,128)S(1)}, f32[4,2,2,16]{3,2,0,1:T(2,128)S(1)}, u32[]{:S(2)}, u32[]{:S(2)}) collective-permute-start(f32[4,2,2,16]{3,2,0,1:T(2,128)S(1)} %collective-permute-done.20), channel_id=1, source_target_pairs={{0,1},{1,2},{2,3},{3,4},{4,5},{5,6},{6,7},{7,8},{8,9},{9,10},{10,1... | collective-permute-start | bytes 3080 | tf_op jit(solution)/shard_map/ppermute | solution.py:24
  216.1 7.0 %collective-permute-start.28 = (f32[4,2,2,16]{3,2,0,1:T(2,128)S(1)}, f32[4,2,2,16]{3,2,0,1:T(2,128)S(1)}, u32[]{:S(2)}, u32[]{:S(2)}) collective-permute-start(f32[4,2,2,16]{3,2,0,1:T(2,128)S(1)} %collective-permute-done.27), channel_id=1, source_target_pairs={{1,0},{2,1},{3,2},{4,3},{5,4},{6,5},{7,6},{8,7},{9,8},{10,9},{11,1... | collective-permute-start | bytes 3080 | tf_op jit(solution)/shard_map/ppermute | solution.py:26
  221.7 5.9 %collective-permute-start.22 = (f32[4,2,2,16]{3,2,0,1:T(2,128)S(1)}, f32[4,2,2,16]{3,2,0,1:T(2,128)S(1)}, u32[]{:S(2)}, u32[]{:S(2)}) collective-permute-start(f32[4,2,2,16]{3,2,0,1:T(2,128)S(1)} %collective-permute-done.21), channel_id=1, source_target_pairs={{0,1},{1,2},{2,3},{3,4},{4,5},{5,6},{6,7},{7,8},{8,9},{9,10},{10,1... | collective-permute-start | bytes 3080 | tf_op jit(solution)/shard_map/ppermute | solution.py:24
  223.1 5.9 %collective-permute-start.29 = (f32[4,2,2,16]{3,2,0,1:T(2,128)S(1)}, f32[4,2,2,16]{3,2,0,1:T(2,128)S(1)}, u32[]{:S(2)}, u32[]{:S(2)}) collective-permute-start(f32[4,2,2,16]{3,2,0,1:T(2,128)S(1)} %collective-permute-done.28), channel_id=1, source_target_pairs={{1,0},{2,1},{3,2},{4,3},{5,4},{6,5},{7,6},{8,7},{9,8},{10,9},{11,1... | collective-permute-start | bytes 3080 | tf_op jit(solution)/shard_map/ppermute | solution.py:26
  227.6 5.8 %collective-permute-start.23 = (f32[4,2,2,16]{3,2,0,1:T(2,128)S(1)}, f32[4,2,2,16]{3,2,0,1:T(2,128)S(1)}, u32[]{:S(2)}, u32[]{:S(2)}) collective-permute-start(f32[4,2,2,16]{3,2,0,1:T(2,128)S(1)} %collective-permute-done.22), channel_id=1, source_target_pairs={{0,1},{1,2},{2,3},{3,4},{4,5},{5,6},{6,7},{7,8},{8,9},{9,10},{10,1... | collective-permute-start | bytes 3080 | tf_op jit(solution)/shard_map/ppermute | solution.py:24
  229.0 10.6 %collective-permute-start.30 = (f32[4,2,2,16]{3,2,0,1:T(2,128)S(1)}, f32[4,2,2,16]{3,2,0,1:T(2,128)S(1)}, u32[]{:S(2)}, u32[]{:S(2)}) collective-permute-start(f32[4,2,2,16]{3,2,0,1:T(2,128)S(1)} %collective-permute-done.29), channel_id=1, source_target_pairs={{1,0},{2,1},{3,2},{4,3},{5,4},{6,5},{7,6},{8,7},{9,8},{10,9},{11,1... | collective-permute-start | bytes 3080 | tf_op jit(solution)/shard_map/ppermute | solution.py:26
  233.4 10.6 %collective-permute-start.24 = (f32[4,2,2,16]{3,2,0,1:T(2,128)S(1)}, f32[4,2,2,16]{3,2,0,1:T(2,128)S(1)}, u32[]{:S(2)}, u32[]{:S(2)}) collective-permute-start(f32[4,2,2,16]{3,2,0,1:T(2,128)S(1)} %collective-permute-done.23), channel_id=1, source_target_pairs={{0,1},{1,2},{2,3},{3,4},{4,5},{5,6},{6,7},{7,8},{8,9},{9,10},{10,1... | collective-permute-start | bytes 3080 | tf_op jit(solution)/shard_map/ppermute | solution.py:24
  239.6 5.8 %collective-permute-start.31 = (f32[4,2,2,16]{3,2,0,1:T(2,128)S(1)}, f32[4,2,2,16]{3,2,0,1:T(2,128)S(1)}, u32[]{:S(2)}, u32[]{:S(2)}) collective-permute-start(f32[4,2,2,16]{3,2,0,1:T(2,128)S(1)} %collective-permute-done.30), channel_id=1, source_target_pairs={{1,0},{2,1},{3,2},{4,3},{5,4},{6,5},{7,6},{8,7},{9,8},{10,9},{11,1... | collective-permute-start | bytes 3080 | tf_op jit(solution)/shard_map/ppermute | solution.py:26
  244.0 5.8 %collective-permute-start.25 = (f32[4,2,2,16]{3,2,0,1:T(2,128)S(1)}, f32[4,2,2,16]{3,2,0,1:T(2,128)S(1)}, u32[]{:S(2)}, u32[]{:S(2)}) collective-permute-start(f32[4,2,2,16]{3,2,0,1:T(2,128)S(1)} %collective-permute-done.24), channel_id=1, source_target_pairs={{0,1},{1,2},{2,3},{3,4},{4,5},{5,6},{6,7},{7,8},{8,9},{9,10},{10,1... | collective-permute-start | bytes 3080 | tf_op jit(solution)/shard_map/ppermute | solution.py:24
  245.3 5.8 %collective-permute-start.32 = (f32[4,2,2,16]{3,2,0,1:T(2,128)S(1)}, f32[4,2,2,16]{3,2,0,1:T(2,128)S(1)}, u32[]{:S(2)}, u32[]{:S(2)}) collective-permute-start(f32[4,2,2,16]{3,2,0,1:T(2,128)S(1)} %collective-permute-done.31), channel_id=1, source_target_pairs={{1,0},{2,1},{3,2},{4,3},{5,4},{6,5},{7,6},{8,7},{9,8},{10,9},{11,1... | collective-permute-start | bytes 3080 | tf_op jit(solution)/shard_map/ppermute | solution.py:26
  251.1 13.4 %collective-permute-start.33 = (f32[4,2,2,16]{3,2,0,1:T(2,128)S(1)}, f32[4,2,2,16]{3,2,0,1:T(2,128)S(1)}, u32[]{:S(2)}, u32[]{:S(2)}) collective-permute-start(f32[4,2,2,16]{3,2,0,1:T(2,128)S(1)} %collective-permute-done.32), channel_id=1, source_target_pairs={{1,0},{2,1},{3,2},{4,3},{5,4},{6,5},{7,6},{8,7},{9,8},{10,9},{11,1... | collective-permute-start | bytes 3080 | tf_op jit(solution)/shard_map/ppermute | solution.py:26
  (18 other events, 387.6 us)
